TPU v7x, 32 devices: a whole 2x2x4 slice. The times are simulated.
32 devices in a mesh: group: 2 (over x), head: 16 (over z, y, core).
Axes of the slice: x: 2, y: 2, z: 4, core: 2. Of those that a mesh axis runs over, the one named last changes fastest.
Arguments:
- queries: bfloat16 [4096, 64, 192], P(('group', 'head')), parts along dimension 0, may hold values from -20 to 20
- latent: bfloat16 [4096, 512], P(('group', 'head')), parts along dimension 0, may hold values from -6 to 6
- rope_key: bfloat16 [4096, 64], P(('group', 'head')), parts along dimension 0, may hold values from -8 to 8
- key_up: bfloat16 [512, 64, 128], P(None, 'head'), may hold values from -0.25 to 0.25
- value_up: bfloat16 [512, 64, 128], P(None, 'head'), may hold values from -0.25 to 0.25
- first_key: int32 [4096], P('group'), parts along dimension 0, may hold values from 0 to 2047, as said below
- out_grad: bfloat16 [4096, 64, 128], P(('group', 'head')), parts along dimension 0, may hold values from -6 to 6
Outputs:
- query_grad: bfloat16 [4096, 64, 192], P(('group', 'head')), parts along dimension 0
- latent_grad: bfloat16 [4096, 512], P(('group', 'head')), parts along dimension 0
- rope_key_grad: bfloat16 [4096, 64], P(('group', 'head')), parts along dimension 0
- key_up_grad: float32 [1024, 64, 128], P('group', 'head'), parts along dimension 0
- value_up_grad: float32 [1024, 64, 128], P('group', 'head'), parts along dimension 0
There are 2 independent parts, one for each index of `group`. A program takes and returns all parts, laid end to end along the dimension named above; an argument that names none is the same for every part. Nothing has to cross between parts.
Inputs may be any that keep to these rules, and one draw needn't show every extreme that they name: first_key never decreases as i grows, first_key[i] <= i, and i - first_key[i] < 512.
All inputs are finite; a program needn't handle non-finite values.
Results may differ from a plain program's by a relative error of at most 0.024.
Values may be sent and summed in bfloat16 or wider, within the bound.
No kernel may reach another device: no remote copies, remote signals or barrier semaphores. Data moves between devices by JAX's collectives and lax.ppermute only.
A program may use at most 128 MiB of HBM per device.

v0:
```python
import math

import jax
import jax.numpy as jnp
from jax import lax
from jax.sharding import PartitionSpec as P


def expand(latent_all, key_up, value_up):
    key_nope = jnp.einsum(
        "tc,chd->thd", latent_all, key_up, preferred_element_type=jnp.float32
    ).astype(jnp.bfloat16)
    values = jnp.einsum(
        "tc,chd->thd", latent_all, value_up, preferred_element_type=jnp.float32
    ).astype(jnp.bfloat16)
    return (key_nope, values)


def shards(queries, latent, rope_key, key_up, value_up, first_key, out_grad):
    wide = jnp.float32
    low = jnp.bfloat16
    own_rows = queries.shape[0]
    devices = lax.axis_size("head")
    seq_len = own_rows * devices
    local_heads = key_up.shape[1]
    nope_width = key_up.shape[2]
    qk_width = queries.shape[2]
    value_width = out_grad.shape[2]
    score_scale = 1.0 / math.sqrt(qk_width)
    query_all, grad_all = (
        lax.all_to_all(queries, "head", split_axis=1, concat_axis=0, tiled=True),
        lax.all_to_all(out_grad, "head", split_axis=1, concat_axis=0, tiled=True),
    )
    latent_all, rope_all = (
        lax.all_gather(latent, "head", axis=0, tiled=True),
        lax.all_gather(rope_key, "head", axis=0, tiled=True),
    )
    key_nope, values = expand(latent_all, key_up, value_up)
    keys_all = jnp.concatenate(
        [
            key_nope,
            jnp.broadcast_to(rope_all[:, None, :], (seq_len, local_heads, rope_all.shape[1])),
        ],
        axis=2,
    )
    query_rows = 4 * own_rows
    reach = 4 * own_rows
    window = query_rows + reach
    block_count = seq_len // query_rows

    def backward_block(block_index, carry):
        query_grad, key_grad, value_grad = carry
        first_row = block_index * query_rows
        first_col = jnp.maximum(first_row - reach, 0)
        query_block = lax.dynamic_slice_in_dim(query_all, first_row, query_rows, 0)
        grad_block = lax.dynamic_slice_in_dim(grad_all, first_row, query_rows, 0)
        key_block = lax.dynamic_slice_in_dim(keys_all, first_col, window, 0)
        value_block = lax.dynamic_slice_in_dim(values, first_col, window, 0)
        limits = lax.dynamic_slice_in_dim(first_key, first_row, query_rows, 0)
        row_pos = first_row + jnp.arange(query_rows, dtype=jnp.int32)
        col_pos = first_col + jnp.arange(window, dtype=jnp.int32)
        visible = (col_pos[None, :] >= limits[:, None]) & (col_pos[None, :] <= row_pos[:, None])
        scores = (
            jnp.einsum("ihd,jhd->hij", query_block, key_block, preferred_element_type=wide)
            * score_scale
        )
        scores = jnp.where(visible[None], scores, -jnp.inf)
        peak = jnp.max(scores, axis=2, keepdims=True)
        log_total = peak + jnp.log(jnp.sum(jnp.exp(scores - peak), axis=2, keepdims=True))
        probs = jnp.exp(scores - log_total)
        probs_low = probs.astype(low)
        attended = jnp.einsum("hij,jhd->ihd", probs_low, value_block, preferred_element_type=wide)
        delta = jnp.sum(grad_block.astype(wide) * attended, axis=2).T[:, :, None]
        prob_grad = jnp.einsum("ihd,jhd->hij", grad_block, value_block, preferred_element_type=wide)
        score_grad = (probs * (prob_grad - delta)).astype(low)
        block_qgrad = (
            score_scale
            * jnp.einsum("hij,jhd->ihd", score_grad, key_block, preferred_element_type=wide)
        ).astype(low)
        block_kgrad = score_scale * jnp.einsum(
            "hij,ihd->jhd", score_grad, query_block, preferred_element_type=wide
        )
        block_vgrad = jnp.einsum("hij,ihd->jhd", probs_low, grad_block, preferred_element_type=wide)
        query_grad = lax.dynamic_update_slice_in_dim(query_grad, block_qgrad, first_row, 0)
        key_grad = lax.dynamic_update_slice_in_dim(
            key_grad,
            lax.dynamic_slice_in_dim(key_grad, first_col, window, 0) + block_kgrad,
            first_col,
            0,
        )
        value_grad = lax.dynamic_update_slice_in_dim(
            value_grad,
            lax.dynamic_slice_in_dim(value_grad, first_col, window, 0) + block_vgrad,
            first_col,
            0,
        )
        return (query_grad, key_grad, value_grad)

    start = (
        jnp.zeros((seq_len, local_heads, qk_width), low),
        jnp.zeros((seq_len, local_heads, qk_width), wide),
        jnp.zeros((seq_len, local_heads, value_width), wide),
    )
    query_grad, key_grad, value_grad = lax.fori_loop(0, block_count, backward_block, start)
    key_low = key_grad.astype(low)
    value_low = value_grad.astype(low)
    key_part = key_low[:, :, :nope_width]
    key_up_grad = jnp.einsum("tc,thd->chd", latent_all, key_part, preferred_element_type=wide)
    value_up_grad = jnp.einsum("tc,thd->chd", latent_all, value_low, preferred_element_type=wide)
    query_out = lax.all_to_all(query_grad, "head", split_axis=0, concat_axis=1, tiled=True)
    latent_part = jnp.einsum(
        "thd,chd->tc", key_part, key_up, preferred_element_type=wide
    ) + jnp.einsum("thd,chd->tc", value_low, value_up, preferred_element_type=wide)
    rope_part = jnp.sum(key_low[:, :, nope_width:].astype(wide), axis=1)
    latent_sum, rope_sum = (
        lax.psum_scatter(
            latent_part.astype(jnp.bfloat16), "head", scatter_dimension=0, tiled=True
        ).astype(jnp.float32),
        lax.psum_scatter(
            rope_part.astype(jnp.bfloat16), "head", scatter_dimension=0, tiled=True
        ).astype(jnp.float32),
    )
    return (query_out, latent_sum.astype(low), rope_sum.astype(low), key_up_grad, value_up_grad)


def solution(mesh):
    return jax.shard_map(
        shards,
        mesh=mesh,
        in_specs=(
            P(("group", "head"), None, None),
            P(("group", "head"), None),
            P(("group", "head"), None),
            P(None, "head", None),
            P(None, "head", None),
            P("group"),
            P(("group", "head"), None, None),
        ),
        out_specs=(
            P(("group", "head"), None, None),
            P(("group", "head"), None),
            P(("group", "head"), None),
            P("group", "head", None),
            P("group", "head", None),
        ),
        check_vma=False,
    )
```

profile of v0, /device:TPU:0, one launch (start us, length us, event | category | flops | bytes accessed | tf_op | source)
XLA Modules:
  0.0 623.6 jit_solution(4153530364047778592)
XLA Ops:
  10.2 54.4 %all_to_all.54 = bf16[128,64,128]{2,0,1:T(8,128)(2,1)S(1)} all-to-all(bf16[128,64,128]{2,0,1:T(8,128)(2,1)S(1)} %copy.32), channel_id=1, replica_groups=mesh['group'=2,'head'=16] {'head'}, dimensions={1} | all-to-all | bytes 4194304 | tf_op jit(solution)/shard_map/all_to_all | solution.py:32
  64.6 5.3 all-to-all-start
  72.0 78.8 %all_gather.7 = bf16[2048,64]{0,1:T(8,128)(2,1)S(1)} all-gather(bf16[128,64]{0,1:T(8,128)(2,1)S(1)} %copy-done.10), channel_id=1, replica_groups=mesh['group'=2,'head'=16] {'head'}, dimensions={0}, use_global_device_ids=true | all-gather | bytes 278528 | tf_op jit(solution)/shard_map/all_gather | solution.py:36
  160.2 5.6 copy.57
  165.8 5.8 all_to_all.42
  179.5 250.4 %while.19 = (s32[]{:T(128)}, bf16[2048,4,192]{0,2,1:T(8,128)(2,1)}, f32[2048,4,192]{0,2,1:T(8,128)}, f32[2048,4,128]{0,2,1:T(8,128)}, bf16[2048,4,192]{0,2,1:T(8...) while((s32[]{:T(128)}, bf16[2048,4,192]{0,2,1:T(8,128)(2,1)}, ...), condition=%wide.region_4.5_spmd, body=%wide.region_0.4_spmd.sunk | while | flops 4075812352 | bytes 215853504 | solution.py:104
  194.0 10.4 %dynamic_update_slice.36 = f32[2048,4,128]{0,2,1:T(8,128)} dynamic-update-slice(f32[2048,4,128]{0,2,1:T(8,128)} %get-tuple-element.336, f32[1024,4,128]{0,2,1:T(8,128)S(1)} %bitcast_add_fusion.6, s32[]{:T(128)S(6)} %max.11, s32[]{:T(128)} %constant.80.clone.1..sunk, s32[]{:T(128)} %constant.80.clone.1..sunk) | dynamic-update-slice | bytes 4194308 | tf_op jit(solution)/shard_map/while/body/eval_jaxpr/dynamic_update_slice | solution.py:91
  204.4 6.3 %fusion.78 = f32[512,4]{0,1:T(4,128)S(1)} fusion(bf16[2048,4,128]{2,0,1:T(8,128)(2,1)} %get-tuple-element.355, s32[]{:T(128)S(6)} %max.11, bf16[2048,4,128]{2,0,1:T(8,128)(2,1)} %get-tuple-element.354, s32[]{:T(128)S(6)} %select_n.54, f32[4,512,1024]{2,1,0:T(8,128)} %copy-done.2, f32[4,512]{1,0:T(4,128)S(1)} %log_add_fusion.2, ...), kind=kOutput, calls=%fused_computation.17.clone.1 | convolution fusion | flops 546043904 | bytes 10502152 | tf_op jit(solution)/shard_map/while/body/eval_jaxpr/hij,jhd->ihd/dot_general | solution.py:72
  211.2 4.5 multiply_convert_fusion.3
  221.9 15.7 %dynamic_update_slice.35 = f32[2048,4,192]{0,2,1:T(8,128)} dynamic-update-slice(f32[2048,4,192]{0,2,1:T(8,128)} %get-tuple-element.335, f32[1024,4,192]{0,2,1:T(8,128)} %bitcast_add_fusion.5, s32[]{:T(128)S(6)} %max.11, s32[]{:T(128)} %constant.80.clone.1..sunk, s32[]{:T(128)} %constant.80.clone.1..sunk) | dynamic-update-slice | bytes 6291460 | tf_op jit(solution)/shard_map/while/body/eval_jaxpr/dynamic_update_slice | solution.py:85
  237.5 5.2 fusion.79
  257.2 10.4 %dynamic_update_slice.36 = f32[2048,4,128]{0,2,1:T(8,128)} dynamic-update-slice(f32[2048,4,128]{0,2,1:T(8,128)} %get-tuple-element.336, f32[1024,4,128]{0,2,1:T(8,128)S(1)} %bitcast_add_fusion.6, s32[]{:T(128)S(6)} %max.11, s32[]{:T(128)} %constant.80.clone.1..sunk, s32[]{:T(128)} %constant.80.clone.1..sunk) | dynamic-update-slice | bytes 4194308 | tf_op jit(solution)/shard_map/while/body/eval_jaxpr/dynamic_update_slice | solution.py:91
  267.5 6.3 %fusion.78 = f32[512,4]{0,1:T(4,128)S(1)} fusion(bf16[2048,4,128]{2,0,1:T(8,128)(2,1)} %get-tuple-element.355, s32[]{:T(128)S(6)} %max.11, bf16[2048,4,128]{2,0,1:T(8,128)(2,1)} %get-tuple-element.354, s32[]{:T(128)S(6)} %select_n.54, f32[4,512,1024]{2,1,0:T(8,128)} %copy-done.2, f32[4,512]{1,0:T(4,128)S(1)} %log_add_fusion.2, ...), kind=kOutput, calls=%fused_computation.17.clone.1 | convolution fusion | flops 546043904 | bytes 10502152 | tf_op jit(solution)/shard_map/while/body/eval_jaxpr/hij,jhd->ihd/dot_general | solution.py:72
  274.3 4.5 multiply_convert_fusion.3
  285.0 15.7 %dynamic_update_slice.35 = f32[2048,4,192]{0,2,1:T(8,128)} dynamic-update-slice(f32[2048,4,192]{0,2,1:T(8,128)} %get-tuple-element.335, f32[1024,4,192]{0,2,1:T(8,128)} %bitcast_add_fusion.5, s32[]{:T(128)S(6)} %max.11, s32[]{:T(128)} %constant.80.clone.1..sunk, s32[]{:T(128)} %constant.80.clone.1..sunk) | dynamic-update-slice | bytes 6291460 | tf_op jit(solution)/shard_map/while/body/eval_jaxpr/dynamic_update_slice | solution.py:85
  300.7 5.2 fusion.79
  320.3 10.1 %dynamic_update_slice.36 = f32[2048,4,128]{0,2,1:T(8,128)} dynamic-update-slice(f32[2048,4,128]{0,2,1:T(8,128)} %get-tuple-element.336, f32[1024,4,128]{0,2,1:T(8,128)S(1)} %bitcast_add_fusion.6, s32[]{:T(128)S(6)} %max.11, s32[]{:T(128)} %constant.80.clone.1..sunk, s32[]{:T(128)} %constant.80.clone.1..sunk) | dynamic-update-slice | bytes 4194308 | tf_op jit(solution)/shard_map/while/body/eval_jaxpr/dynamic_update_slice | solution.py:91
  330.5 6.3 %fusion.78 = f32[512,4]{0,1:T(4,128)S(1)} fusion(bf16[2048,4,128]{2,0,1:T(8,128)(2,1)} %get-tuple-element.355, s32[]{:T(128)S(6)} %max.11, bf16[2048,4,128]{2,0,1:T(8,128)(2,1)} %get-tuple-element.354, s32[]{:T(128)S(6)} %select_n.54, f32[4,512,1024]{2,1,0:T(8,128)} %copy-done.2, f32[4,512]{1,0:T(4,128)S(1)} %log_add_fusion.2, ...), kind=kOutput, calls=%fused_computation.17.clone.1 | convolution fusion | flops 546043904 | bytes 10502152 | tf_op jit(solution)/shard_map/while/body/eval_jaxpr/hij,jhd->ihd/dot_general | solution.py:72
  337.3 4.5 multiply_convert_fusion.3
  347.9 15.5 %dynamic_update_slice.35 = f32[2048,4,192]{0,2,1:T(8,128)} dynamic-update-slice(f32[2048,4,192]{0,2,1:T(8,128)} %get-tuple-element.335, f32[1024,4,192]{0,2,1:T(8,128)} %bitcast_add_fusion.5, s32[]{:T(128)S(6)} %max.11, s32[]{:T(128)} %constant.80.clone.1..sunk, s32[]{:T(128)} %constant.80.clone.1..sunk) | dynamic-update-slice | bytes 6291460 | tf_op jit(solution)/shard_map/while/body/eval_jaxpr/dynamic_update_slice | solution.py:85
  363.4 5.2 fusion.79
  383.0 9.5 %dynamic_update_slice.36 = f32[2048,4,128]{0,2,1:T(8,128)} dynamic-update-slice(f32[2048,4,128]{0,2,1:T(8,128)} %get-tuple-element.336, f32[1024,4,128]{0,2,1:T(8,128)S(1)} %bitcast_add_fusion.6, s32[]{:T(128)S(6)} %max.11, s32[]{:T(128)} %constant.80.clone.1..sunk, s32[]{:T(128)} %constant.80.clone.1..sunk) | dynamic-update-slice | bytes 4194308 | tf_op jit(solution)/shard_map/while/body/eval_jaxpr/dynamic_update_slice | solution.py:91
  392.5 6.3 %fusion.78 = f32[512,4]{0,1:T(4,128)S(1)} fusion(bf16[2048,4,128]{2,0,1:T(8,128)(2,1)} %get-tuple-element.355, s32[]{:T(128)S(6)} %max.11, bf16[2048,4,128]{2,0,1:T(8,128)(2,1)} %get-tuple-element.354, s32[]{:T(128)S(6)} %select_n.54, f32[4,512,1024]{2,1,0:T(8,128)} %copy-done.2, f32[4,512]{1,0:T(4,128)S(1)} %log_add_fusion.2, ...), kind=kOutput, calls=%fused_computation.17.clone.1 | convolution fusion | flops 546043904 | bytes 10502152 | tf_op jit(solution)/shard_map/while/body/eval_jaxpr/hij,jhd->ihd/dot_general | solution.py:72
  399.3 4.5 multiply_convert_fusion.3
  410.0 14.9 %dynamic_update_slice.35 = f32[2048,4,192]{0,2,1:T(8,128)} dynamic-update-slice(f32[2048,4,192]{0,2,1:T(8,128)} %get-tuple-element.335, f32[1024,4,192]{0,2,1:T(8,128)} %bitcast_add_fusion.5, s32[]{:T(128)S(6)} %max.11, s32[]{:T(128)} %constant.80.clone.1..sunk, s32[]{:T(128)} %constant.80.clone.1..sunk) | dynamic-update-slice | bytes 6291460 | tf_op jit(solution)/shard_map/while/body/eval_jaxpr/dynamic_update_slice | solution.py:85
  424.8 5.1 fusion.79
  429.9 7.2 %copy.35 = bf16[2048,4,192]{2,1,0:T(4,128)(2,1)} copy(bf16[2048,4,192]{0,2,1:T(8,128)(2,1)} %get-tuple-element.227) | data formatting | bytes 6291456 | tf_op jit(solution)/shard_map/while | solution.py:104
  437.1 16.9 %all-to-all-start.2 = ((bf16[2048,4,192]{2,1,0:T(4,128)(2,1)}), bf16[2048,4,192]{2,1,0:T(4,128)(2,1)}, u32[]{:S(2)}, u32[]{:S(2)}) async-start(bf16[2048,4,192]{2,1,0:T(4,128)(2,1)} %copy.35), calls=%async_computation.2 | async-start | bytes 8388608 | tf_op jit(solution)/shard_map/all_to_all | solution.py:110
  454.1 6.7 %copy.37 = bf16[2048,4,192]{2,0,1:T(8,128)(2,1)} copy(f32[2048,4,192]{0,2,1:T(8,128)} %get-tuple-element.228) | data formatting | bytes 9437184 | tf_op jit(solution)/shard_map/while | solution.py:104
  483.0 63.3 %reduce-scatter.7.cloned.1.call-done = bf16[128,64]{1,0:T(8,128)(2,1)} async-done(((bf16[2048,64]{1,0:T(8,128)(2,1)}), bf16[128,64]{1,0:T(8,128)(2,1)}) %reduce-scatter.7.cloned.1.call-update) | async-done | bytes 16400
  547.8 7.1 %copy.36 = bf16[128,16,4,192]{0,3,2,1:T(8,128)(2,1)} copy(bf16[128,16,4,192]{3,2,0,1:T(4,128)(2,1)} %bitcast.14) | data formatting | bytes 6291456 | tf_op jit(solution)/shard_map/all_to_all | solution.py:110
  554.9 62.2 %reduce-scatter.5.cloned.1.call-done = bf16[128,512]{1,0:T(8,128)(2,1)} async-done(((bf16[2048,512]{1,0:T(8,128)(2,1)}), bf16[128,512]{1,0:T(8,128)(2,1)}) %reduce-scatter.5.cloned.1.call-update) | async-done | bytes 131088 | tf_op jit(solution)/shard_map/reduce_scatter | solution.py:116
  (138 shorter events, 130.5 us)
Async XLA Ops:
  7.2 150.2 %copy-start = (bf16[512,4,128]{2,1,0:T(4,128)(2,1)S(1)}, bf16[512,4,128]{2,1,0:T(4,128)(2,1)}, u32[]{:S(2)}) copy-start(bf16[512,4,128]{2,1,0:T(4,128)(2,1)} %param.13) | copy-start | bytes 1572868
  64.6 7.4 %copy-start.10 = (bf16[128,64]{0,1:T(8,128)(2,1)S(1)}, bf16[128,64]{0,1:T(8,128)(2,1)}, u32[]{:S(2)}) copy-start(bf16[128,64]{0,1:T(8,128)(2,1)} %param.11) | copy-start | bytes 49156
  64.6 95.6 %all-to-all-start = ((bf16[128,64,192]{0,2,1:T(8,128)(2,1)}), bf16[128,64,192]{0,2,1:T(8,128)(2,1)}, u32[]{:S(2)}, u32[]{:S(2)}) async-start(bf16[128,64,192]{0,2,1:T(8,128)(2,1)} %param.9), calls=%async_computation | async-start | bytes 6291456 | tf_op jit(solution)/shard_map/all_to_all | solution.py:31
  69.9 80.8 %all-gather.2.cloned.1.call-start = ((), (), s32[]{:S(2)}) async-start(), calls=%async_computation.5 | async-start | bytes 2228224 | tf_op jit(solution)/shard_map/all_gather | solution.py:35
  71.9 81.7 %copy-start.8 = (bf16[512,4,128]{0,2,1:T(8,128)(2,1)}, bf16[512,4,128]{0,2,1:T(8,128)(2,1)S(1)}, u32[]{:S(2)}) copy-start(bf16[512,4,128]{0,2,1:T(8,128)(2,1)S(1)} %copy.30) | copy-start | bytes 1572868
  185.0 4.3 copy-start.2
  185.0 5.2 copy-start.4
  204.4 6.3 %copy-start.3 = (f32[4,512,1024]{2,1,0:T(8,128)S(1)}, f32[4,512,1024]{2,1,0:T(8,128)}, u32[]{:S(2)}) copy-start(f32[4,512,1024]{2,1,0:T(8,128)} %copy-done.2) | copy-start | bytes 25165828 | tf_op jit(solution)/shard_map/while
  204.4 6.8 %copy-start.11 = (bf16[2048,4,128]{2,0,1:T(8,128)(2,1)S(1)}, bf16[2048,4,128]{2,0,1:T(8,128)(2,1)}, u32[]{:S(2)}) copy-start(bf16[2048,4,128]{2,0,1:T(8,128)(2,1)} %get-tuple-element.355) | copy-start | bytes 6291460 | tf_op jit(solution)/shard_map/while
  204.4 13.4 %slice-start = ((s8[6291456]{0:T(1024)(128)(4,1)}), s8[4194304]{0:T(1024)(128)(4,1)S(1)}, s32[]{:S(2)}) async-start(s8[6291456]{0:T(1024)(128)(4,1)} %bitcast.74), calls=%async_computation.8 | async-start | bytes 8388608 | tf_op jit(solution)/shard_map/while
  211.2 6.6 %slice-start.1 = ((s8[6291456]{0:T(1024)(128)(4,1)}), s8[2097152]{0:T(1024)(128)(4,1)S(1)}, s32[]{:S(2)}) async-start(s8[6291456]{0:T(1024)(128)(4,1)} %bitcast.74), calls=%async_computation.9 | async-start | bytes 4194304 | tf_op jit(solution)/shard_map/while
  248.2 5.2 copy-start.4
  267.5 6.3 %copy-start.3 = (f32[4,512,1024]{2,1,0:T(8,128)S(1)}, f32[4,512,1024]{2,1,0:T(8,128)}, u32[]{:S(2)}) copy-start(f32[4,512,1024]{2,1,0:T(8,128)} %copy-done.2) | copy-start | bytes 25165828 | tf_op jit(solution)/shard_map/while
  267.5 6.8 %copy-start.11 = (bf16[2048,4,128]{2,0,1:T(8,128)(2,1)S(1)}, bf16[2048,4,128]{2,0,1:T(8,128)(2,1)}, u32[]{:S(2)}) copy-start(bf16[2048,4,128]{2,0,1:T(8,128)(2,1)} %get-tuple-element.355) | copy-start | bytes 6291460 | tf_op jit(solution)/shard_map/while
  267.5 13.4 %slice-start = ((s8[6291456]{0:T(1024)(128)(4,1)}), s8[4194304]{0:T(1024)(128)(4,1)S(1)}, s32[]{:S(2)}) async-start(s8[6291456]{0:T(1024)(128)(4,1)} %bitcast.74), calls=%async_computation.8 | async-start | bytes 8388608 | tf_op jit(solution)/shard_map/while
  274.3 6.6 %slice-start.1 = ((s8[6291456]{0:T(1024)(128)(4,1)}), s8[2097152]{0:T(1024)(128)(4,1)S(1)}, s32[]{:S(2)}) async-start(s8[6291456]{0:T(1024)(128)(4,1)} %bitcast.74), calls=%async_computation.9 | async-start | bytes 4194304 | tf_op jit(solution)/shard_map/while
  311.3 4.3 copy-start.2
  311.3 5.2 copy-start.4
  330.4 6.3 %copy-start.3 = (f32[4,512,1024]{2,1,0:T(8,128)S(1)}, f32[4,512,1024]{2,1,0:T(8,128)}, u32[]{:S(2)}) copy-start(f32[4,512,1024]{2,1,0:T(8,128)} %copy-done.2) | copy-start | bytes 25165828 | tf_op jit(solution)/shard_map/while
  330.4 6.8 %copy-start.11 = (bf16[2048,4,128]{2,0,1:T(8,128)(2,1)S(1)}, bf16[2048,4,128]{2,0,1:T(8,128)(2,1)}, u32[]{:S(2)}) copy-start(bf16[2048,4,128]{2,0,1:T(8,128)(2,1)} %get-tuple-element.355) | copy-start | bytes 6291460 | tf_op jit(solution)/shard_map/while
  330.4 13.4 %slice-start = ((s8[6291456]{0:T(1024)(128)(4,1)}), s8[4194304]{0:T(1024)(128)(4,1)S(1)}, s32[]{:S(2)}) async-start(s8[6291456]{0:T(1024)(128)(4,1)} %bitcast.74), calls=%async_computation.8 | async-start | bytes 8388608 | tf_op jit(solution)/shard_map/while
  337.3 6.5 %slice-start.1 = ((s8[6291456]{0:T(1024)(128)(4,1)}), s8[2097152]{0:T(1024)(128)(4,1)S(1)}, s32[]{:S(2)}) async-start(s8[6291456]{0:T(1024)(128)(4,1)} %bitcast.74), calls=%async_computation.9 | async-start | bytes 4194304 | tf_op jit(solution)/shard_map/while
  374.0 4.3 copy-start.2
  374.0 5.2 copy-start.4
  392.5 6.3 %copy-start.3 = (f32[4,512,1024]{2,1,0:T(8,128)S(1)}, f32[4,512,1024]{2,1,0:T(8,128)}, u32[]{:S(2)}) copy-start(f32[4,512,1024]{2,1,0:T(8,128)} %copy-done.2) | copy-start | bytes 25165828 | tf_op jit(solution)/shard_map/while
  392.5 6.8 %copy-start.11 = (bf16[2048,4,128]{2,0,1:T(8,128)(2,1)S(1)}, bf16[2048,4,128]{2,0,1:T(8,128)(2,1)}, u32[]{:S(2)}) copy-start(bf16[2048,4,128]{2,0,1:T(8,128)(2,1)} %get-tuple-element.355) | copy-start | bytes 6291460 | tf_op jit(solution)/shard_map/while
  392.5 13.3 %slice-start = ((s8[6291456]{0:T(1024)(128)(4,1)}), s8[4194304]{0:T(1024)(128)(4,1)S(1)}, s32[]{:S(2)}) async-start(s8[6291456]{0:T(1024)(128)(4,1)} %bitcast.74), calls=%async_computation.8 | async-start | bytes 8388608 | tf_op jit(solution)/shard_map/while
  399.3 6.5 %slice-start.1 = ((s8[6291456]{0:T(1024)(128)(4,1)}), s8[2097152]{0:T(1024)(128)(4,1)S(1)}, s32[]{:S(2)}) async-start(s8[6291456]{0:T(1024)(128)(4,1)} %bitcast.74), calls=%async_computation.9 | async-start | bytes 4194304 | tf_op jit(solution)/shard_map/while
  437.1 110.7 %all-to-all-start.2 = ((bf16[2048,4,192]{2,1,0:T(4,128)(2,1)}), bf16[2048,4,192]{2,1,0:T(4,128)(2,1)}, u32[]{:S(2)}, u32[]{:S(2)}) async-start(bf16[2048,4,192]{2,1,0:T(4,128)(2,1)} %copy.35), calls=%async_computation.2 | async-start | bytes 8388608 | tf_op jit(solution)/shard_map/all_to_all | solution.py:110
  454.0 92.3 %reduce-scatter.7.cloned.1.call-start = ((), (), s32[]{:S(2)}) async-start(), calls=%async_computation.7 | async-start | bytes 557056
  454.1 9.8 %copy-start.9 = (bf16[512,4,128]{0,2,1:T(8,128)(2,1)S(1)}, bf16[512,4,128]{0,2,1:T(8,128)(2,1)}, u32[]{:S(2)}) copy-start(bf16[512,4,128]{0,2,1:T(8,128)(2,1)} %copy-done.8) | copy-start | bytes 1572868
  463.8 153.2 %reduce-scatter.5.cloned.1.call-start = ((), (), s32[]{:S(2)}) async-start(), calls=%async_computation.6 | async-start | bytes 2228224 | tf_op jit(solution)/shard_map/reduce_scatter | solution.py:116
  (8 other events, 20.3 us)
Sparse Core Ops, SparseCore 0:
  72.9 66.9 all-gather.1
  464.0 82.2 reduce-scatter.6
  550.6 66.3 reduce-scatter.4
where the time goes:
time: 628 us; the launch traced here: 624 us
  local copies, waits for them, and re-layouts  179 us (29%)
  blocking collectives  133 us (21%)
  matrix products  131 us (21%)
  waiting for transfers between devices  126 us (20%)
  starting transfers between devices  22.4 us (4%)
  other arithmetic  17 us (3%)
  between operations  13.9 us (2%)
    all_gather x1, blocking collectives, shards(): lax.all_gather(rope_key, 'head', axis=0, tiled=True)  78.8 us
    unnamed x4, waiting for transfers between devices  64 us
    reduce_scatter x1, waiting for transfers between devices, shards(): lax.psum_scatter(latent_part.astype(jnp.bfloat16), 'head', scatter_dimens...  62.2 us
    dynamic_update_slice x4, local copies, waits for them, and re-layouts, backward_block(): lax.dynamic_update_slice_in_dim(key_grad, lax.dynamic_slice_in_dim(key_gr...  61.6 us
    all_to_all x1, blocking collectives, shards(): lax.all_to_all(out_grad, 'head', split_axis=1, concat_axis=0, tiled=True)  54.4 us
    dynamic_update_slice x4, local copies, waits for them, and re-layouts, backward_block(): lax.dynamic_update_slice_in_dim(value_grad, lax.dynamic_slice_in_dim(valu...  40.3 us
    dot_general x4, matrix products, backward_block(): jnp.einsum('hij,jhd->ihd', probs_low, value_block, preferred_element_type...  25.1 us
    while x56, local copies, waits for them, and re-layouts  21.2 us
  transfers between devices with their start and end apart: 5, of which 2 were waited for; matrix products, arithmetic and copies ran while one was open for 8% of the time, Pallas kernels for 0%

commit v1 on v0

v1 whole, which is shorter than its diff:
```python
import functools
import math

import jax
import jax.numpy as jnp
from jax import lax
from jax.experimental import pallas as pl
from jax.experimental.pallas import tpu as pltpu
from jax.sharding import PartitionSpec as P

WIDE = jnp.float32
LOW = jnp.bfloat16
PLANE = 4
NT = (((1,), (1,)), ((), ()))
NN = (((1,), (0,)), ((), ()))


def dot(a, b, dims):
    return lax.dot_general(a, b, dims, preferred_element_type=WIDE)


def step_kernel(
    heads, nope, rope, vd, rows,
    pos_ref, x0, x1, x2, x3, w_ref, latr_ref, latt_ref, first_ref, dlat_in,
    y0, y1, y2, y3, dw_ref, dlat_ref,
    q_s, do_s, k_s, v_s, kt_s, dk_s, dv_s, dq_s, bias_s, dkb_s, dvb_s,
):
    width = latt_ref.shape[0]
    qk = nope + rope
    scale = 1.0 / math.sqrt(qk)
    keys = latr_ref.shape[0]
    block = first_ref.shape[2]
    blocks = first_ref.shape[0]
    reach = keys - block * blocks
    window = reach + block
    place = pos_ref[0]
    hn, hv = heads * nope, heads * vd

    for k, x in enumerate((x0, x1, x2, x3)):
        at = pl.ds(pl.multiple_of((place ^ k) * rows, rows), rows)
        for h in range(heads):
            q_s[h, at, :nope] = x[:, h * nope:(h + 1) * nope]
            q_s[h, at, nope:] = x[:, hn + hv + h * rope:hn + hv + (h + 1) * rope]
            do_s[h, at, :] = x[:, hn + h * vd:hn + (h + 1) * vd]

    lat = latr_ref[:, :width]
    key_rope = latr_ref[:, width:]
    key_nope = dot(lat, w_ref[:, :hn], NN).astype(LOW)
    for h in range(heads):
        k_s[h, :, :nope] = key_nope[:, h * nope:(h + 1) * nope]
        k_s[h, :, nope:] = key_rope
    values = dot(lat, w_ref[:, hn:], NN).astype(LOW)
    for h in range(heads):
        v_s[h] = values[:, h * vd:(h + 1) * vd]
    for h in range(heads):
        kt_s[h] = k_s[h].T

    dk_s[...] = jnp.zeros_like(dk_s)
    dv_s[...] = jnp.zeros_like(dv_s)

    for b in range(blocks):
        col = b * block + lax.broadcasted_iota(jnp.int32, (window, block), 0)
        row = b * block + reach + lax.broadcasted_iota(jnp.int32, (window, block), 1)
        seen = (col >= first_ref[b]) & (col <= row)
        bias_s[b] = jnp.where(seen, 0.0, -1e30)

    def attend(i, carry):
        h = i // blocks
        b = i % blocks
        mine = pl.ds(pl.multiple_of(b * block, block), block)
        near = pl.ds(pl.multiple_of(b * block, block), window)
        q = q_s[h, mine, :]
        do = do_s[h, mine, :]
        kw = k_s[h, near, :]
        vw = v_s[h, near, :]
        t = dot(kw, q, NT) * (scale * math.log2(math.e)) + bias_s[b]
        peak = jnp.max(t, axis=0, keepdims=True)
        e = jnp.exp2(t - peak)
        inv = 1.0 / jnp.sum(e, axis=0, keepdims=True)
        probs = e * inv
        dp = dot(vw, do, NT)
        delta = jnp.sum(probs * dp, axis=0, keepdims=True)
        ds = (probs * (dp - delta)).astype(LOW)
        dv_s[h, near, :] += dot(probs.astype(LOW), do, NN)
        dk_s[h, near, :] += dot(ds, q, NN)
        dqt = dot(kt_s[h, :, near], ds, NN) * scale
        dq_s[h, mine, :] = dqt.T.astype(LOW)
        return carry

    lax.fori_loop(0, heads * blocks, attend, 0)

    rope_sum = dlat_in[:, width:]
    for h in range(heads):
        dkh = (dk_s[h] * scale).astype(LOW)
        dkb_s[:, h * nope:(h + 1) * nope] = dkh[:, :nope]
        rope_sum = rope_sum + dkh[:, nope:].astype(WIDE)
        dvb_s[:, h * vd:(h + 1) * vd] = dv_s[h].astype(LOW)
    dlat_ref[:, width:] = rope_sum
    dw_ref[:, :hn] = dot(latt_ref[...], dkb_s[...], NN)
    dw_ref[:, hn:] = dot(latt_ref[...], dvb_s[...], NN)
    dlat_ref[:, :width] = (
        dlat_in[:, :width]
        + dot(dkb_s[...], w_ref[:, :hn], NT)
        + dot(dvb_s[...], w_ref[:, hn:], NT)
    )
    for k, y in enumerate((y0, y1, y2, y3)):
        at = pl.ds(pl.multiple_of((place ^ k) * rows, rows), rows)
        for h in range(heads):
            y[:, h * nope:(h + 1) * nope] = dq_s[h, at, :nope]
            y[:, hn + h * rope:hn + (h + 1) * rope] = dq_s[h, at, nope:]


def attention_step(pos, xs, w, latr, latt, first, dlat, heads, nope, rope, vd):
    rows = xs[0].shape[0]
    keys, both = latr.shape
    width = latt.shape[0]
    blocks, _, block = first.shape
    queries = blocks * block
    window = keys - queries + block
    qk = nope + rope
    vmem = pl.BlockSpec(memory_space=pltpu.VMEM)
    flops = 2 * heads * blocks * block * window * (3 * qk + 2 * vd)
    flops += 6 * keys * width * heads * (nope + vd)
    return pl.pallas_call(
        functools.partial(step_kernel, heads, nope, rope, vd, rows),
        name="attention_step",
        in_specs=[pl.BlockSpec(memory_space=pltpu.SMEM)] + [vmem] * 9,
        out_specs=[vmem] * 6,
        out_shape=[jax.ShapeDtypeStruct((rows, heads * qk), LOW)] * 4
        + [
            jax.ShapeDtypeStruct((width, heads * (nope + vd)), WIDE),
            jax.ShapeDtypeStruct((keys, both), WIDE),
        ],
        scratch_shapes=[
            pltpu.VMEM((heads, queries, qk), LOW),
            pltpu.VMEM((heads, queries, vd), LOW),
            pltpu.VMEM((heads, keys, qk), LOW),
            pltpu.VMEM((heads, keys, vd), LOW),
            pltpu.VMEM((heads, qk, keys), LOW),
            pltpu.VMEM((heads, keys, qk), WIDE),
            pltpu.VMEM((heads, keys, vd), WIDE),
            pltpu.VMEM((heads, queries, qk), LOW),
            pltpu.VMEM((blocks, window, block), WIDE),
            pltpu.VMEM((keys, heads * nope), LOW),
            pltpu.VMEM((keys, heads * vd), LOW),
        ],
        input_output_aliases={9: 5},
        compiler_params=pltpu.CompilerParams(vmem_limit_bytes=50 << 20),
        cost_estimate=pl.CostEstimate(
            flops=flops,
            bytes_accessed=12 << 20,
            transcendentals=heads * blocks * block * window,
        ),
    )(pos, *xs, w, latr, latt, first, dlat)


def shards(queries, latent, rope_key, key_up, value_up, first_key, out_grad):
    rows, all_heads, qk = queries.shape
    devices = lax.axis_size("head")
    width, heads, nope = key_up.shape
    vd = out_grad.shape[2]
    rope = qk - nope
    planes = devices // PLANE
    span = PLANE * rows
    me = lax.axis_index("head")
    plane, place = me // PLANE, me % PLANE
    onward = [(d, (d + PLANE) % devices) for d in range(devices)]
    back = [(d, (d - PLANE) % devices) for d in range(devices)]
    swaps = [[(d, d ^ k) for d in range(devices)] for k in range(PLANE)]

    def swap(value, k):
        return lax.ppermute(value, "head", swaps[k]) if k else value

    def pick(value, index):
        return lax.dynamic_index_in_dim(value, index, 0, keepdims=False)

    weights = [
        jnp.concatenate(
            [key_up.reshape(width, heads * nope), value_up.reshape(width, heads * vd)], axis=1
        )
    ]
    for _ in range(planes - 1):
        weights.append(lax.ppermute(weights[-1], "head", onward))

    own = jnp.concatenate([latent, rope_key], axis=1)
    pair = jnp.stack([lax.ppermute(own, "head", onward), own])
    around = jnp.stack([swap(pair, k) for k in range(PLANE)])
    latr = jnp.concatenate([pick(around, place ^ b) for b in range(PLANE)], axis=1)
    latr = latr.reshape(2 * span, width + rope)
    latt = latr[:, :width].T

    def spread(value):
        return value.reshape(rows, planes, PLANE, -1).transpose(1, 2, 0, 3)

    sends = jnp.concatenate(
        [spread(queries[:, :, :nope]), spread(out_grad), spread(queries[:, :, nope:])], axis=3
    )
    first = lax.dynamic_slice_in_dim(first_key, plane * span, span, 0) - (plane - 1) * span
    first = first.reshape(2, 1, span // 2)
    pos = place.reshape(1).astype(jnp.int32)

    dlat = jnp.zeros((2 * span, width + rope), WIDE)
    grads = jnp.zeros((planes, PLANE, rows, heads * qk), LOW)
    total = None
    mine = None
    order = list(range(1, planes - 1)) + [0, planes - 1]
    for s in order:
        owner = (plane - s) % planes
        chunk = pick(sends, owner)
        xs = [swap(pick(chunk, place ^ k), k) for k in range(PLANE)]
        out = attention_step(
            pos, xs, weights[s], latr, latt, first, dlat, heads, nope, rope, vd
        )
        ys, dw, dlat = out[:4], out[4], out[5]
        for k in range(PLANE):
            grads = lax.dynamic_update_slice(
                grads, swap(ys[k], k)[None, None], (owner, place ^ k, 0, 0)
            )
        if s == 0:
            mine = dw
        else:
            total = dw.astype(LOW) if total is None else (total.astype(WIDE) + dw).astype(LOW)
            total = lax.ppermute(total, "head", onward)

    dw = mine + total.astype(WIDE)
    key_up_grad = dw[:, :heads * nope].reshape(width, heads, nope)
    value_up_grad = dw[:, heads * nope:].reshape(width, heads, vd)

    def gather(value, w):
        return value.transpose(2, 0, 1, 3).reshape(rows, all_heads, w)

    query_out = jnp.concatenate(
        [gather(grads[..., :heads * nope], nope), gather(grads[..., heads * nope:], rope)], axis=2
    )

    part = dlat.astype(LOW).reshape(2, PLANE, rows, width + rope).transpose(1, 0, 2, 3)
    summed = 0.0
    for k in range(PLANE):
        summed = summed + swap(pick(part, place ^ k), k).astype(WIDE)
    moved = lax.ppermute(summed[0].astype(LOW), "head", back).astype(WIDE)
    lat_sum = summed[1] + jnp.where(plane < planes - 1, moved, 0.0)
    lat_sum = lat_sum.astype(LOW)
    return (query_out, lat_sum[:, :width], lat_sum[:, width:], key_up_grad, value_up_grad)


def solution(mesh):
    return jax.shard_map(
        shards,
        mesh=mesh,
        in_specs=(
            P(("group", "head"), None, None),
            P(("group", "head"), None),
            P(("group", "head"), None),
            P(None, "head", None),
            P(None, "head", None),
            P("group"),
            P(("group", "head"), None, None),
        ),
        out_specs=(
            P(("group", "head"), None, None),
            P(("group", "head"), None),
            P(("group", "head"), None),
            P("group", "head", None),
            P("group", "head", None),
        ),
        check_vma=False,
    )
```

time: 628 us -> 257 us (0.41)
  blocking collectives: 133 us -> 0 us
  matrix products: 131 us -> 0 us
  local copies, waits for them, and re-layouts: 179 us -> 53 us
  Pallas kernels: 0 us -> 77.4 us
  waiting for transfers between devices: 126 us -> 67.5 us
  starting transfers between devices: 22.4 us -> 37.8 us
  between operations: 13.9 us -> 1.03 us
    dot_general x29 -> x0, matrix products: 129 us -> none  [the longest x4 25.1 us: backward_block(): jnp.einsum('hij,jhd->ihd', probs_low, value_block, preferred_element_type...]
    dynamic_update_slice x8 -> x17, local copies, waits for them, and re-layouts: 102 us -> 7.65 us  [shards(): lax.dynamic_update_slice(grads, swap(ys[k], k)[None, None], (owner, place...]
    all_gather x1 -> x0, blocking collectives: 78.8 us -> none  [shards(): lax.all_gather(rope_key, 'head', axis=0, tiled=True)]
    pallas_call x0 -> x4, Pallas kernels: none -> 77.4 us  [attention_step(): pl.pallas_call(functools.partial(step_kernel, heads, nope, rope, vd, rows...]
    ppermute x0 -> x38, waiting for transfers between devices: none -> 67.5 us  [the longest x30 62.6 us: swap(): return lax.ppermute(value, 'head', swaps[k]) if k else value]
    unnamed x4 -> x0, waiting for transfers between devices: 64 us -> none
    reduce_scatter x1 -> x0, waiting for transfers between devices: 62.2 us -> none  [shards(): lax.psum_scatter(latent_part.astype(jnp.bfloat16), 'head', scatter_dimens...]
    all_to_all x1 -> x0, blocking collectives: 54.4 us -> none  [shards(): lax.all_to_all(out_grad, 'head', split_axis=1, concat_axis=0, tiled=True)]
  transfers between devices with their start and end apart: 5 -> 38, of which waited for: 2 -> 16; matrix products, arithmetic and copies ran while one was open for 8% -> 25% of each run, Pallas kernels for 0% -> 30%
where the time goes in v1:
time: 257 us
  Pallas kernels  77.4 us (30%)
  waiting for transfers between devices  67.5 us (26%)
  local copies, waits for them, and re-layouts  53 us (21%)
  starting transfers between devices  37.8 us (15%)
  other arithmetic  19.9 us (8%)
    pallas_call x4, Pallas kernels, attention_step(): pl.pallas_call(functools.partial(step_kernel, heads, nope, rope, vd, rows...  77.4 us
    ppermute x30, waiting for transfers between devices, swap(): return lax.ppermute(value, 'head', swaps[k]) if k else value  62.6 us
    ppermute x30, starting transfers between devices, swap(): return lax.ppermute(value, 'head', swaps[k]) if k else value  23.8 us
    reshape x4, local copies, waits for them, and re-layouts, spread(): return value.reshape(rows, planes, PLANE, -1).transpose(1, 2, 0, 3)  13.8 us
    dynamic_update_slice x17, local copies, waits for them, and re-layouts, shards(): lax.dynamic_update_slice(grads, swap(ys[k], k)[None, None], (owner, place...  7.65 us
  transfers between devices with their start and end apart: 38, of which 16 were waited for; matrix products, arithmetic and copies ran while one was open for 25% of the time, Pallas kernels for 30%

profile of v1, /device:TPU:0, one launch (start us, length us, event | category | flops | bytes accessed | tf_op | source)
XLA Modules:
  0.0 256.6 jit_solution(867013961863376189)
XLA Ops:
  3.1 3.1 %collective-permute-start.4 = (bf16[128,576]{0,1:T(8,128)(2,1)}, bf16[128,576]{0,1:T(8,128)(2,1)S(1)}, u32[]{:S(2)}, u32[]{:S(2)}) collective-permute-start(bf16[128,576]{0,1:T(8,128)(2,1)} %get-tuple-element.96), channel_id=1, source_target_pairs={{0,4},{1,5},{2,6},{3,7},{4,8},{5,9},{6,10},{7,11},{8,12},{9,13},{1... | collective-permute-start | bytes 442376 | tf_op jit(solution)/shard_map/ppermute | solution.py:186
  10.0 3.2 %slice.34 = bf16[128,64,128]{0,2,1:T(8,128)(2,1)} slice(bf16[128,64,192]{0,2,1:T(8,128)(2,1)} %param.7), slice={[0:128], [0:64], [0:128]} | slice | bytes 4194304 | tf_op jit(solution)/shard_map/slice | solution.py:196
  13.2 2.3 slice.35
  15.5 4.1 %reshape.94 = bf16[128,4,4,512]{3,2,1,0:T(4,128)(2,1)} reshape(bf16[128,64,128]{2,1,0:T(8,128)(2,1)} %param.13) | data formatting | bytes 4194304 | tf_op jit(solution)/shard_map/reshape | solution.py:193
  19.6 4.1 %copy.71 = bf16[128,4,4,512]{3,0,2,1:T(8,128)(2,1)} copy(bf16[128,4,4,512]{3,2,1,0:T(4,128)(2,1)} %reshape.94) | data formatting | bytes 4194304 | tf_op jit(solution)/shard_map/reshape | solution.py:193
  23.7 4.1 %copy.47 = bf16[128,4,4,512]{3,0,2,1:T(8,128)(2,1)} copy(bf16[128,4,4,512]{0,3,2,1:T(8,128)(2,1)} %bitcast.129) | data formatting | bytes 4194304 | tf_op jit(solution)/shard_map/reshape | solution.py:193
  29.3 5.1 %pad_maximum_fusion = bf16[4,4,128,1280]{3,2,1,0:T(8,128)(2,1)} fusion(bf16[4,4,128,256]{3,2,1,0:T(8,128)(2,1)S(1)} %bitcast.131, bf16[4,4,128,512]{3,2,1,0:T(8,128)(2,1)} %bitcast.127, bf16[4,4,128,512]{3,2,1,0:T(8,128)(2,1)} %bitcast.128), kind=kLoop, calls=%fused_computation | loop fusion | flops 15728640 | bytes 10485760 | tf_op jit(solution)/shard_map/concatenate | solution.py:195
  37.1 4.4 %dynamic-slice_bitcast_fusion = (bf16[128,1280]{1,0:T(8,128)(2,1)}, bf16[128,1280]{1,0:T(8,128)(2,1)}, bf16[128,1280]{1,0:T(8,128)(2,1)}, bf16[128,1280]{1,0:T(8...) fusion(bf16[4,4,128,1280]{3,2,1,0:T(8,128)(2,1)} %pad_maximum_f, ...), kind=kLoop, calls=%fused_computation.14 | loop fusion | bytes 10485792 | tf_op jit(solution)/shard_map/jit(dynamic_index_in_dim)/squeeze | solution.py:175
  45.8 5.1 %collective-permute-done.7 = bf16[2,128,576]{1,2,0:T(8,128)(2,1)} collective-permute-done((bf16[2,128,576]{1,2,0:T(8,128)(2,1)}, bf16[2,128,576]{1,2,0:T(8,128)(2,1)}, u32[]{:S(2)}, u32[]{:S(2)}) %collective-permute-start.7) | collective-permute-done | bytes 294944 | tf_op jit(solution)/shard_map/ppermute | solution.py:172
  54.4 2.4 copy.53.latr_ref
  56.8 2.3 slice_bitcast_fusion.latt_ref
  60.6 4.3 %collective-permute-done.2.x3 = bf16[128,1280]{1,0:T(8,128)(2,1)} collective-permute-done((bf16[128,1280]{1,0:T(8,128)(2,1)}, bf16[128,1280]{1,0:T(8,128)(2,1)}, u32[]{:S(2)}, u32[]{:S(2)}) %collective-permute-start.2) | collective-permute-done | bytes 327712 | tf_op jit(solution)/shard_map/ppermute | solution.py:172
  66.6 19.6 %attention_step.4 = (bf16[128,768]{1,0:T(8,128)(2,1)S(1)}, bf16[128,768]{1,0:T(8,128)(2,1)S(1)}, bf16[128,768]{1,0:T(8,128)(2,1)S(1)}, bf16[128,768]{1,0:T(8,128...) custom-call(s32[1]{0:T(128)} %bitcast.pos_ref, ...), custom_call_target="tpu_custom_call", output_to_operand_aliasing={{5}: (9, {})} | custom-call | flops 5838471168 | bytes 12582912 | tf_op jit(solution)/shard_map/attention_step/pallas_call | solution.py:124
  92.6 5.2 %collective-permute-done.9 = bf16[128,768]{1,0:T(8,128)(2,1)S(1)} collective-permute-done((bf16[128,768]{1,0:T(8,128)(2,1)S(1)}, bf16[128,768]{1,0:T(8,128)(2,1)S(1)}, u32[]{:S(2)}, u32[]{:S(2)}) %collective-permute-start.9) | collective-permute-done | bytes 196640 | tf_op jit(solution)/shard_map/ppermute | solution.py:172
  101.0 2.2 collective-permute-start.13
  103.4 5.6 %collective-permute-done.12.x2 = bf16[128,1280]{1,0:T(8,128)(2,1)S(1)} collective-permute-done((bf16[128,1280]{1,0:T(8,128)(2,1)S(1)}, bf16[128,1280]{1,0:T(8,128)(2,1)S(1)}, u32[]{:S(2)}, u32[]{:S(2)}) %collective-permute-start.12) | collective-permute-done | bytes 327712 | tf_op jit(solution)/shard_map/ppermute | solution.py:172
  110.5 4.5 %collective-permute-done.13.x3 = bf16[128,1280]{1,0:T(8,128)(2,1)S(1)} collective-permute-done((bf16[128,1280]{1,0:T(8,128)(2,1)S(1)}, bf16[128,1280]{1,0:T(8,128)(2,1)S(1)}, u32[]{:S(2)}, u32[]{:S(2)}) %collective-permute-start.13) | collective-permute-done | bytes 327712 | tf_op jit(solution)/shard_map/ppermute | solution.py:172
  115.1 1.9 collective-permute-start.20
  117.0 19.4 %attention_step.5 = (bf16[128,768]{1,0:T(8,128)(2,1)S(1)}, bf16[128,768]{1,0:T(8,128)(2,1)S(1)}, bf16[128,768]{1,0:T(8,128)(2,1)S(1)}, bf16[128,768]{1,0:T(8,128...) custom-call(s32[1]{0:T(128)} %bitcast.pos_ref, ...), custom_call_target="tpu_custom_call", output_to_operand_aliasing={{5}: (9, {})} | custom-call | flops 5838471168 | bytes 12582912 | tf_op jit(solution)/shard_map/attention_step/pallas_call | solution.py:124
  136.3 1.9 add_convert_fusion.1
  140.6 19.2 %attention_step.6 = (bf16[128,768]{1,0:T(8,128)(2,1)S(1)}, bf16[128,768]{1,0:T(8,128)(2,1)S(1)}, bf16[128,768]{1,0:T(8,128)(2,1)S(1)}, bf16[128,768]{1,0:T(8,128...) custom-call(s32[1]{0:T(128)} %bitcast.pos_ref, ...), custom_call_target="tpu_custom_call", output_to_operand_aliasing={{5}: (9, {})} | custom-call | flops 5838471168 | bytes 12582912 | tf_op jit(solution)/shard_map/attention_step/pallas_call | solution.py:124
  163.5 4.8 %collective-permute-done.22 = bf16[128,768]{1,0:T(8,128)(2,1)S(1)} collective-permute-done((bf16[128,768]{1,0:T(8,128)(2,1)S(1)}, bf16[128,768]{1,0:T(8,128)(2,1)S(1)}, u32[]{:S(2)}, u32[]{:S(2)}) %collective-permute-start.22) | collective-permute-done | bytes 196640 | tf_op jit(solution)/shard_map/ppermute | solution.py:172
  168.3 2.3 collective-permute-done.23
  172.3 7.2 %collective-permute-done.25.x2 = bf16[128,1280]{1,0:T(8,128)(2,1)S(1)} collective-permute-done((bf16[128,1280]{1,0:T(8,128)(2,1)S(1)}, bf16[128,1280]{1,0:T(8,128)(2,1)S(1)}, u32[]{:S(2)}, u32[]{:S(2)}) %collective-permute-start.25) | collective-permute-done | bytes 327712 | tf_op jit(solution)/shard_map/ppermute | solution.py:172
  179.5 5.1 %collective-permute-done.26.x3 = bf16[128,1280]{1,0:T(8,128)(2,1)S(1)} collective-permute-done((bf16[128,1280]{1,0:T(8,128)(2,1)S(1)}, bf16[128,1280]{1,0:T(8,128)(2,1)S(1)}, u32[]{:S(2)}, u32[]{:S(2)}) %collective-permute-start.26) | collective-permute-done | bytes 327712 | tf_op jit(solution)/shard_map/ppermute | solution.py:172
  184.7 3.5 %collective-permute-done.27.w_ref = bf16[512,1024]{1,0:T(8,128)(2,1)S(1)} collective-permute-done((bf16[512,1024]{1,0:T(8,128)(2,1)S(1)}, bf16[512,1024]{1,0:T(8,128)(2,1)S(1)}, u32[]{:S(2)}, u32[]{:S(2)}) %collective-permute-start.27) | collective-permute-done | bytes 1048608 | tf_op jit(solution)/shard_map/ppermute | solution.py:183
  188.2 19.3 %attention_step.7 = (bf16[128,768]{1,0:T(8,128)(2,1)S(1)}, bf16[128,768]{1,0:T(8,128)(2,1)S(1)}, bf16[128,768]{1,0:T(8,128)(2,1)S(1)}, bf16[128,768]{1,0:T(8,128...) custom-call(s32[1]{0:T(128)} %bitcast.pos_ref, ...), custom_call_target="tpu_custom_call", output_to_operand_aliasing={{5}: (9, {})} | custom-call | flops 5838471168 | bytes 12582912 | tf_op jit(solution)/shard_map/attention_step/pallas_call | solution.py:124
  207.5 3.1 %add_convert_fusion = bf16[512,1024]{1,0:T(8,128)(2,1)} fusion(f32[512,1024]{1,0:T(8,128)} %get-tuple-element.52, bf16[512,1024]{1,0:T(8,128)(2,1)S(1)} %collective-permute-done.36), kind=kLoop, calls=%fused_computation.4 | loop fusion | flops 1572864 | bytes 4194304 | tf_op jit(solution)/shard_map/convert_element_type | solution.py:222
  219.1 13.7 %collective-permute-done.29 = bf16[128,768]{1,0:T(8,128)(2,1)S(1)} collective-permute-done((bf16[128,768]{1,0:T(8,128)(2,1)S(1)}, bf16[128,768]{1,0:T(8,128)(2,1)S(1)}, u32[]{:S(2)}, u32[]{:S(2)}) %collective-permute-start.29) | collective-permute-done | bytes 196640 | tf_op jit(solution)/shard_map/ppermute | solution.py:172
  234.0 4.6 %copy.57 = bf16[4,4,128,768]{2,3,1,0:T(8,128)(2,1)} copy(bf16[4,4,128,768]{3,2,1,0:T(8,128)(2,1)} %bitcast_dynamic-update-slice_fusion.2) | data formatting | bytes 6291456 | tf_op jit(solution)/shard_map/dynamic_update_slice | solution.py:216
  244.9 3.9 %collective-permute-start.34 = (bf16[128,576]{0,1:T(8,128)(2,1)S(1)}, bf16[128,576]{0,1:T(8,128)(2,1)S(1)}, u32[]{:S(2)}, u32[]{:S(2)}) collective-permute-start(bf16[128,576]{0,1:T(8,128)(2,1)S(1)} %fusion.4), channel_id=1, source_target_pairs={{0,12},{1,13},{2,14},{3,15},{4,0},{5,1},{6,2},{7,3},{8,4},{9,5},{1... | collective-permute-start | bytes 442376 | tf_op jit(solution)/shard_map/ppermute | solution.py:240
  248.8 1.9 pad_maximum_fusion.1
  (132 shorter events, 62.3 us)
Async XLA Ops:
  3.1 31.3 %collective-permute-start.4 = (bf16[128,576]{0,1:T(8,128)(2,1)}, bf16[128,576]{0,1:T(8,128)(2,1)S(1)}, u32[]{:S(2)}, u32[]{:S(2)}) collective-permute-start(bf16[128,576]{0,1:T(8,128)(2,1)} %get-tuple-element.96), channel_id=1, source_target_pairs={{0,4},{1,5},{2,6},{3,7},{4,8},{5,9},{6,10},{7,11},{8,12},{9,13},{1... | collective-permute-start | bytes 442376 | tf_op jit(solution)/shard_map/ppermute | solution.py:186
  8.4 50.7 %collective-permute-start.3 = (bf16[512,1024]{1,0:T(8,128)(2,1)S(1)}, bf16[512,1024]{1,0:T(8,128)(2,1)S(1)}, u32[]{:S(2)}, u32[]{:S(2)}) collective-permute-start(bf16[512,1024]{1,0:T(8,128)(2,1)S(1)} %bitcast_dynamic-update-slice_fusion.w_ref), channel_id=1, source_target_pairs={{0,4},{1,5},{2,6},{3,7},{4,8},{5,9},{6,10},{7,11},{8,12},{9,13},{1... | collective-permute-start | bytes 3145736 | tf_op jit(solution)/shard_map/ppermute | solution.py:183
  35.3 10.2 %collective-permute-start.6 = (bf16[2,128,576]{1,2,0:T(8,128)(2,1)}, bf16[2,128,576]{1,2,0:T(8,128)(2,1)}, u32[]{:S(2)}, u32[]{:S(2)}) collective-permute-start(bf16[2,128,576]{1,2,0:T(8,128)(2,1)} %get-tuple-element.95), channel_id=1, source_target_pairs={{0,2},{1,3},{2,0},{3,1},{4,6},{5,7},{6,4},{7,5},{8,10},{9,11},{10,... | collective-permute-start | bytes 884744 | tf_op jit(solution)/shard_map/ppermute | solution.py:172
  36.8 14.1 %collective-permute-start.7 = (bf16[2,128,576]{1,2,0:T(8,128)(2,1)}, bf16[2,128,576]{1,2,0:T(8,128)(2,1)}, u32[]{:S(2)}, u32[]{:S(2)}) collective-permute-start(bf16[2,128,576]{1,2,0:T(8,128)(2,1)} %get-tuple-element.95), channel_id=1, source_target_pairs={{0,3},{1,2},{2,1},{3,0},{4,7},{5,6},{6,5},{7,4},{8,11},{9,10},{10,... | collective-permute-start | bytes 884744 | tf_op jit(solution)/shard_map/ppermute | solution.py:172
  41.5 19.1 %collective-permute-start = (bf16[128,1280]{1,0:T(8,128)(2,1)}, bf16[128,1280]{1,0:T(8,128)(2,1)}, u32[]{:S(2)}, u32[]{:S(2)}) collective-permute-start(bf16[128,1280]{1,0:T(8,128)(2,1)} %get-tuple-element.82), channel_id=1, source_target_pairs={{0,1},{1,0},{2,3},{3,2},{4,5},{5,4},{6,7},{7,6},{8,9},{9,8},{10,11... | collective-permute-start | bytes 983048 | tf_op jit(solution)/shard_map/ppermute | solution.py:172
  42.6 18.0 %collective-permute-start.1 = (bf16[128,1280]{1,0:T(8,128)(2,1)}, bf16[128,1280]{1,0:T(8,128)(2,1)}, u32[]{:S(2)}, u32[]{:S(2)}) collective-permute-start(bf16[128,1280]{1,0:T(8,128)(2,1)} %get-tuple-element.81), channel_id=1, source_target_pairs={{0,2},{1,3},{2,0},{3,1},{4,6},{5,7},{6,4},{7,5},{8,10},{9,11},{10,... | collective-permute-start | bytes 983048 | tf_op jit(solution)/shard_map/ppermute | solution.py:172
  45.5 19.4 %collective-permute-start.2 = (bf16[128,1280]{1,0:T(8,128)(2,1)}, bf16[128,1280]{1,0:T(8,128)(2,1)}, u32[]{:S(2)}, u32[]{:S(2)}) collective-permute-start(bf16[128,1280]{1,0:T(8,128)(2,1)} %get-tuple-element.80), channel_id=1, source_target_pairs={{0,3},{1,2},{2,1},{3,0},{4,7},{5,6},{6,5},{7,4},{8,11},{9,10},{10,... | collective-permute-start | bytes 983048 | tf_op jit(solution)/shard_map/ppermute | solution.py:172
  50.9 52.4 %collective-permute-start.11 = (bf16[128,1280]{1,0:T(8,128)(2,1)}, bf16[128,1280]{1,0:T(8,128)(2,1)}, u32[]{:S(2)}, u32[]{:S(2)}) collective-permute-start(bf16[128,1280]{1,0:T(8,128)(2,1)} %get-tuple-element.78), channel_id=1, source_target_pairs={{0,1},{1,0},{2,3},{3,2},{4,5},{5,4},{6,7},{7,6},{8,9},{9,8},{10,11... | collective-permute-start | bytes 983048 | tf_op jit(solution)/shard_map/ppermute | solution.py:172
  59.0 57.9 %collective-permute-start.14 = (bf16[512,1024]{1,0:T(8,128)(2,1)S(1)}, bf16[512,1024]{1,0:T(8,128)(2,1)S(1)}, u32[]{:S(2)}, u32[]{:S(2)}) collective-permute-start(bf16[512,1024]{1,0:T(8,128)(2,1)S(1)} %collective-permute-done.3.w_ref), channel_id=1, source_target_pairs={{0,4},{1,5},{2,6},{3,7},{4,8},{5,9},{6,10},{7,11},{8,12},{9,13},{1... | collective-permute-start | bytes 3145736 | tf_op jit(solution)/shard_map/ppermute | solution.py:183
  88.0 48.4 %collective-permute-start.35 = (bf16[512,1024]{1,0:T(8,128)(2,1)S(1)}, bf16[512,1024]{1,0:T(8,128)(2,1)S(1)}, u32[]{:S(2)}, u32[]{:S(2)}) collective-permute-start(bf16[512,1024]{1,0:T(8,128)(2,1)S(1)} %convert_element_type.55), channel_id=1, source_target_pairs={{0,4},{1,5},{2,6},{3,7},{4,8},{5,9},{6,10},{7,11},{8,12},{9,13},{1... | collective-permute-start | bytes 3145736 | tf_op jit(solution)/shard_map/ppermute | solution.py:223
  90.0 7.8 %collective-permute-start.9 = (bf16[128,768]{1,0:T(8,128)(2,1)S(1)}, bf16[128,768]{1,0:T(8,128)(2,1)S(1)}, u32[]{:S(2)}, u32[]{:S(2)}) collective-permute-start(bf16[128,768]{1,0:T(8,128)(2,1)S(1)} %get-tuple-element.31), channel_id=1, source_target_pairs={{0,2},{1,3},{2,0},{3,1},{4,6},{5,7},{6,4},{7,5},{8,10},{9,11},{10,... | collective-permute-start | bytes 589832 | tf_op jit(solution)/shard_map/ppermute | solution.py:172
  91.9 9.2 %collective-permute-start.10 = (bf16[128,768]{1,0:T(8,128)(2,1)S(1)}, bf16[128,768]{1,0:T(8,128)(2,1)S(1)}, u32[]{:S(2)}, u32[]{:S(2)}) collective-permute-start(bf16[128,768]{1,0:T(8,128)(2,1)S(1)} %get-tuple-element.32), channel_id=1, source_target_pairs={{0,3},{1,2},{2,1},{3,0},{4,7},{5,6},{6,5},{7,4},{8,11},{9,10},{10,... | collective-permute-start | bytes 589832 | tf_op jit(solution)/shard_map/ppermute | solution.py:172
  97.8 11.2 %collective-permute-start.12 = (bf16[128,1280]{1,0:T(8,128)(2,1)S(1)}, bf16[128,1280]{1,0:T(8,128)(2,1)S(1)}, u32[]{:S(2)}, u32[]{:S(2)}) collective-permute-start(bf16[128,1280]{1,0:T(8,128)(2,1)S(1)} %copy-done.10), channel_id=1, source_target_pairs={{0,2},{1,3},{2,0},{3,1},{4,6},{5,7},{6,4},{7,5},{8,10},{9,11},{10,... | collective-permute-start | bytes 983048 | tf_op jit(solution)/shard_map/ppermute | solution.py:172
  101.0 14.0 %collective-permute-start.13 = (bf16[128,1280]{1,0:T(8,128)(2,1)S(1)}, bf16[128,1280]{1,0:T(8,128)(2,1)S(1)}, u32[]{:S(2)}, u32[]{:S(2)}) collective-permute-start(bf16[128,1280]{1,0:T(8,128)(2,1)S(1)} %copy-done.9), channel_id=1, source_target_pairs={{0,3},{1,2},{2,1},{3,0},{4,7},{5,6},{6,5},{7,4},{8,11},{9,10},{10,... | collective-permute-start | bytes 983048 | tf_op jit(solution)/shard_map/ppermute | solution.py:172
  103.3 35.4 %collective-permute-start.18 = (bf16[128,1280]{1,0:T(8,128)(2,1)S(1)}, bf16[128,1280]{1,0:T(8,128)(2,1)S(1)}, u32[]{:S(2)}, u32[]{:S(2)}) collective-permute-start(bf16[128,1280]{1,0:T(8,128)(2,1)S(1)} %copy-done.8), channel_id=1, source_target_pairs={{0,1},{1,0},{2,3},{3,2},{4,5},{5,4},{6,7},{7,6},{8,9},{9,8},{10,11... | collective-permute-start | bytes 983048 | tf_op jit(solution)/shard_map/ppermute | solution.py:172
  109.0 29.9 %collective-permute-start.19 = (bf16[128,1280]{1,0:T(8,128)(2,1)S(1)}, bf16[128,1280]{1,0:T(8,128)(2,1)S(1)}, u32[]{:S(2)}, u32[]{:S(2)}) collective-permute-start(bf16[128,1280]{1,0:T(8,128)(2,1)S(1)} %copy-done.7), channel_id=1, source_target_pairs={{0,2},{1,3},{2,0},{3,1},{4,6},{5,7},{6,4},{7,5},{8,10},{9,11},{10,... | collective-permute-start | bytes 983048 | tf_op jit(solution)/shard_map/ppermute | solution.py:172
  115.1 24.4 %collective-permute-start.20 = (bf16[128,1280]{1,0:T(8,128)(2,1)S(1)}, bf16[128,1280]{1,0:T(8,128)(2,1)S(1)}, u32[]{:S(2)}, u32[]{:S(2)}) collective-permute-start(bf16[128,1280]{1,0:T(8,128)(2,1)S(1)} %copy-done.6), channel_id=1, source_target_pairs={{0,3},{1,2},{2,1},{3,0},{4,7},{5,6},{6,5},{7,4},{8,11},{9,10},{10,... | collective-permute-start | bytes 983048 | tf_op jit(solution)/shard_map/ppermute | solution.py:172
  117.0 55.3 %collective-permute-start.24 = (bf16[128,1280]{1,0:T(8,128)(2,1)S(1)}, bf16[128,1280]{1,0:T(8,128)(2,1)S(1)}, u32[]{:S(2)}, u32[]{:S(2)}) collective-permute-start(bf16[128,1280]{1,0:T(8,128)(2,1)S(1)} %copy-done.5), channel_id=1, source_target_pairs={{0,1},{1,0},{2,3},{3,2},{4,5},{5,4},{6,7},{7,6},{8,9},{9,8},{10,11... | collective-permute-start | bytes 983048 | tf_op jit(solution)/shard_map/ppermute | solution.py:172
  138.3 69.2 %collective-permute-start.36 = (bf16[512,1024]{1,0:T(8,128)(2,1)S(1)}, bf16[512,1024]{1,0:T(8,128)(2,1)S(1)}, u32[]{:S(2)}, u32[]{:S(2)}) collective-permute-start(bf16[512,1024]{1,0:T(8,128)(2,1)S(1)} %add_convert_fusion.1), channel_id=1, source_target_pairs={{0,4},{1,5},{2,6},{3,7},{4,8},{5,9},{6,10},{7,11},{8,12},{9,13},{1... | collective-permute-start | bytes 3145736 | tf_op jit(solution)/shard_map/ppermute | solution.py:223
  138.7 21.1 %collective-permute-start.15 = (bf16[128,768]{1,0:T(8,128)(2,1)S(1)}, bf16[128,768]{1,0:T(8,128)(2,1)S(1)}, u32[]{:S(2)}, u32[]{:S(2)}) collective-permute-start(bf16[128,768]{1,0:T(8,128)(2,1)S(1)} %get-tuple-element.35), channel_id=1, source_target_pairs={{0,1},{1,0},{2,3},{3,2},{4,5},{5,4},{6,7},{7,6},{8,9},{9,8},{10,11... | collective-permute-start | bytes 589832 | tf_op jit(solution)/shard_map/ppermute | solution.py:172
  138.9 21.5 %collective-permute-start.16 = (bf16[128,768]{1,0:T(8,128)(2,1)S(1)}, bf16[128,768]{1,0:T(8,128)(2,1)S(1)}, u32[]{:S(2)}, u32[]{:S(2)}) collective-permute-start(bf16[128,768]{1,0:T(8,128)(2,1)S(1)} %get-tuple-element.36), channel_id=1, source_target_pairs={{0,2},{1,3},{2,0},{3,1},{4,6},{5,7},{6,4},{7,5},{8,10},{9,11},{10,... | collective-permute-start | bytes 589832 | tf_op jit(solution)/shard_map/ppermute | solution.py:172
  139.5 21.6 %collective-permute-start.17 = (bf16[128,768]{1,0:T(8,128)(2,1)S(1)}, bf16[128,768]{1,0:T(8,128)(2,1)S(1)}, u32[]{:S(2)}, u32[]{:S(2)}) collective-permute-start(bf16[128,768]{1,0:T(8,128)(2,1)S(1)} %get-tuple-element.37), channel_id=1, source_target_pairs={{0,3},{1,2},{2,1},{3,0},{4,7},{5,6},{6,5},{7,4},{8,11},{9,10},{10,... | collective-permute-start | bytes 589832 | tf_op jit(solution)/shard_map/ppermute | solution.py:172
  160.5 7.8 %collective-permute-start.22 = (bf16[128,768]{1,0:T(8,128)(2,1)S(1)}, bf16[128,768]{1,0:T(8,128)(2,1)S(1)}, u32[]{:S(2)}, u32[]{:S(2)}) collective-permute-start(bf16[128,768]{1,0:T(8,128)(2,1)S(1)} %get-tuple-element.41), channel_id=1, source_target_pairs={{0,2},{1,3},{2,0},{3,1},{4,6},{5,7},{6,4},{7,5},{8,10},{9,11},{10,... | collective-permute-start | bytes 589832 | tf_op jit(solution)/shard_map/ppermute | solution.py:172
  161.1 27.1 %collective-permute-start.27 = (bf16[512,1024]{1,0:T(8,128)(2,1)S(1)}, bf16[512,1024]{1,0:T(8,128)(2,1)S(1)}, u32[]{:S(2)}, u32[]{:S(2)}) collective-permute-start(bf16[512,1024]{1,0:T(8,128)(2,1)S(1)} %collective-permute-done.14.w_ref), channel_id=1, source_target_pairs={{0,4},{1,5},{2,6},{3,7},{4,8},{5,9},{6,10},{7,11},{8,12},{9,13},{1... | collective-permute-start | bytes 3145736 | tf_op jit(solution)/shard_map/ppermute | solution.py:183
  162.8 7.8 %collective-permute-start.23 = (bf16[128,768]{1,0:T(8,128)(2,1)S(1)}, bf16[128,768]{1,0:T(8,128)(2,1)S(1)}, u32[]{:S(2)}, u32[]{:S(2)}) collective-permute-start(bf16[128,768]{1,0:T(8,128)(2,1)S(1)} %get-tuple-element.42), channel_id=1, source_target_pairs={{0,3},{1,2},{2,1},{3,0},{4,7},{5,6},{6,5},{7,4},{8,11},{9,10},{10,... | collective-permute-start | bytes 589832 | tf_op jit(solution)/shard_map/ppermute | solution.py:172
  168.3 11.2 %collective-permute-start.25 = (bf16[128,1280]{1,0:T(8,128)(2,1)S(1)}, bf16[128,1280]{1,0:T(8,128)(2,1)S(1)}, u32[]{:S(2)}, u32[]{:S(2)}) collective-permute-start(bf16[128,1280]{1,0:T(8,128)(2,1)S(1)} %copy-done.4), channel_id=1, source_target_pairs={{0,2},{1,3},{2,0},{3,1},{4,6},{5,7},{6,4},{7,5},{8,10},{9,11},{10,... | collective-permute-start | bytes 983048 | tf_op jit(solution)/shard_map/ppermute | solution.py:172
  170.6 14.0 %collective-permute-start.26 = (bf16[128,1280]{1,0:T(8,128)(2,1)S(1)}, bf16[128,1280]{1,0:T(8,128)(2,1)S(1)}, u32[]{:S(2)}, u32[]{:S(2)}) collective-permute-start(bf16[128,1280]{1,0:T(8,128)(2,1)S(1)} %copy-done.3), channel_id=1, source_target_pairs={{0,3},{1,2},{2,1},{3,0},{4,7},{5,6},{6,5},{7,4},{8,11},{9,10},{10,... | collective-permute-start | bytes 983048 | tf_op jit(solution)/shard_map/ppermute | solution.py:172
  210.5 42.9 %collective-permute-start.37 = (bf16[512,1024]{1,0:T(8,128)(2,1)}, bf16[512,1024]{1,0:T(8,128)(2,1)S(1)}, u32[]{:S(2)}, u32[]{:S(2)}) collective-permute-start(bf16[512,1024]{1,0:T(8,128)(2,1)} %add_convert_fusion), channel_id=1, source_target_pairs={{0,4},{1,5},{2,6},{3,7},{4,8},{5,9},{6,10},{7,11},{8,12},{9,13},{1... | collective-permute-start | bytes 3145736 | tf_op jit(solution)/shard_map/ppermute | solution.py:223
  211.7 32.1 %collective-permute-start.31 = (bf16[2,128,576]{1,2,0:T(8,128)(2,1)}, bf16[2,128,576]{1,2,0:T(8,128)(2,1)S(1)}, u32[]{:S(2)}, u32[]{:S(2)}) collective-permute-start(bf16[2,128,576]{1,2,0:T(8,128)(2,1)} %bitcast.136), channel_id=1, source_target_pairs={{0,1},{1,0},{2,3},{3,2},{4,5},{5,4},{6,7},{7,6},{8,9},{9,8},{10,11... | collective-permute-start | bytes 884744 | tf_op jit(solution)/shard_map/ppermute | solution.py:172
  212.6 31.2 %collective-permute-start.32 = (bf16[2,128,576]{1,2,0:T(8,128)(2,1)}, bf16[2,128,576]{1,2,0:T(8,128)(2,1)S(1)}, u32[]{:S(2)}, u32[]{:S(2)}) collective-permute-start(bf16[2,128,576]{1,2,0:T(8,128)(2,1)} %bitcast.137), channel_id=1, source_target_pairs={{0,2},{1,3},{2,0},{3,1},{4,6},{5,7},{6,4},{7,5},{8,10},{9,11},{10,... | collective-permute-start | bytes 884744 | tf_op jit(solution)/shard_map/ppermute | solution.py:172
  214.8 29.0 %collective-permute-start.33 = (bf16[2,128,576]{1,2,0:T(8,128)(2,1)}, bf16[2,128,576]{1,2,0:T(8,128)(2,1)}, u32[]{:S(2)}, u32[]{:S(2)}) collective-permute-start(bf16[2,128,576]{1,2,0:T(8,128)(2,1)} %bitcast.138), channel_id=1, source_target_pairs={{0,3},{1,2},{2,1},{3,0},{4,7},{5,6},{6,5},{7,4},{8,11},{9,10},{10,... | collective-permute-start | bytes 884744 | tf_op jit(solution)/shard_map/ppermute | solution.py:172
  217.1 15.7 %collective-permute-start.29 = (bf16[128,768]{1,0:T(8,128)(2,1)S(1)}, bf16[128,768]{1,0:T(8,128)(2,1)S(1)}, u32[]{:S(2)}, u32[]{:S(2)}) collective-permute-start(bf16[128,768]{1,0:T(8,128)(2,1)S(1)} %get-tuple-element.46), channel_id=1, source_target_pairs={{0,2},{1,3},{2,0},{3,1},{4,6},{5,7},{6,4},{7,5},{8,10},{9,11},{10,... | collective-permute-start | bytes 589832 | tf_op jit(solution)/shard_map/ppermute | solution.py:172
  (17 other events, 247.8 us)
